TPU v7x, 32 devices: a whole 2x2x4 slice. The times are simulated.
32 devices in a mesh: gx: 2 (over y), gy: 4 (over x, core), gz: 4 (over z).
Axes of the slice: x: 2, y: 2, z: 4, core: 2. Of those that a mesh axis runs over, the one named last changes fastest.
Arguments:
- weights: bfloat16 [2, 216, 16384], P(None, None, ('gx', 'gy', 'gz')), may hold values from -6 to 6
- translate: bfloat16 [2, 2, 216, 216], replicated, may hold values from -0.3125 to 0.3125
- angles: float32 [216, 256], replicated, may hold values from -3.140625 to 3.140625
- box_ids: int32 [5, 16384], P(None, ('gx', 'gy', 'gz')), may hold values from 0 to 255
Outputs:
- transformed: bfloat16 [2, 216, 16384], P(None, None, ('gx', 'gy', 'gz'))
All inputs are finite; a program needn't handle non-finite values.
Results may differ from a plain program's by a relative error of at most 0.018.
Values may be sent and summed in bfloat16 or wider, within the bound.
A program may use at most 64 MiB of HBM per device.

v0:
```python
import jax
import jax.numpy as jnp
from jax import lax
from jax.sharding import PartitionSpec as P


def swapped(block, axis, apart):
    count = lax.axis_size(axis)
    route = []
    for low in range(count):
        high = low | 1 << apart
        if high != low and high < count:
            route += [(low, high), (high, low)]
    return lax.ppermute(block, axis, route)


def rotate(current, labels, cos_tab, sin_tab):
    cosines = jnp.take(cos_tab, labels, axis=1)
    sines = jnp.take(sin_tab, labels, axis=1)
    real_part = current[0].astype(jnp.float32)
    imag_part = current[1].astype(jnp.float32)
    return jnp.stack(
        [cosines * real_part - sines * imag_part, sines * real_part + cosines * imag_part]
    ).astype(jnp.bfloat16)


def combine(kept_half, received, translate, parity):
    own_mats = lax.dynamic_index_in_dim(translate, parity, 1, keepdims=False)
    far_mats = lax.dynamic_index_in_dim(translate, 1 - parity, 1, keepdims=False)
    halves = []
    for target in range(2):
        near_part = jnp.einsum(
            "jk,rkh->rjh", own_mats[target], kept_half, preferred_element_type=jnp.float32
        )
        far_part = jnp.einsum(
            "jk,rkh->rjh", far_mats[target], received, preferred_element_type=jnp.float32
        )
        halves.append(near_part + far_part)
    return jnp.concatenate(halves, axis=2).astype(jnp.bfloat16)


def run_swaps(current, box_ids, level_index, cos_tab, sin_tab, translate, position, extent, mover):
    for bit_no in range(extent.bit_length() - 1):
        rotated = rotate(current, box_ids[level_index], cos_tab, sin_tab)
        parity = jnp.right_shift(position, bit_no) & 1
        half_cols = rotated.shape[2] // 2
        kept_half = lax.dynamic_slice_in_dim(rotated, parity * half_cols, half_cols, 2)
        outgoing = lax.dynamic_slice_in_dim(rotated, (1 - parity) * half_cols, half_cols, 2)
        received = mover(outgoing, bit_no)
        current = combine(kept_half, received, translate, parity)
        level_index += 1
    return (current, level_index)


def shards(weights, translate, angles, box_ids):
    cos_tab = jnp.cos(angles)
    sin_tab = jnp.sin(angles)
    current = weights
    level_index = 0
    current, level_index = run_swaps(
        current,
        box_ids,
        level_index,
        cos_tab,
        sin_tab,
        translate,
        lax.axis_index("gx"),
        lax.axis_size("gx"),
        lambda parcel, which_bit: swapped(parcel, "gx", which_bit),
    )
    current, level_index = run_swaps(
        current,
        box_ids,
        level_index,
        cos_tab,
        sin_tab,
        translate,
        lax.axis_index("gy"),
        lax.axis_size("gy"),
        lambda parcel, which_bit: swapped(parcel, "gy", which_bit),
    )
    current, level_index = run_swaps(
        current,
        box_ids,
        level_index,
        cos_tab,
        sin_tab,
        translate,
        lax.axis_index("gz"),
        lax.axis_size("gz"),
        lambda parcel, which_bit: swapped(parcel, "gz", which_bit),
    )
    return current


def solution(mesh):
    in_specs = (P(None, None, ("gx", "gy", "gz")), P(), P(), P(None, ("gx", "gy", "gz")))
    out_specs = P(None, None, ("gx", "gy", "gz"))
    return jax.shard_map(shards, mesh=mesh, in_specs=in_specs, out_specs=out_specs, check_vma=False)
```

profile of v0, /device:TPU:0, one launch (start us, length us, event | category | flops | bytes accessed | tf_op | source)
XLA Modules:
  0.0 70.7 jit_solution(14181002713032731909)
XLA Ops:
  0.0 0.9 %fusion.113 = (s32[1,512]{1,0:T(1,128)S(1)}, s32[1,512]{1,0:T(1,128)S(1)}, s32[1,512]{1,0:T(1,128)S(1)}, s32[1,512]{1,0:T(1,128)S(1)}, s32[1,512]{1,0:T(1,128)S(1)}) fusion(s32[5,512]{1,0:T(8,128)} %param.9), kind=kLoop, calls=%fused_computation.211 | loop fusion | bytes 20480 | tf_op jit(solution)/shard_map/slice | solution.py:44
  1.0 1.1 %copy.5 = f32[216,256]{0,1:T(8,128)S(1)} copy(f32[216,256]{1,0:T(8,128)} %param.8) | data formatting | bytes 442368 | tf_op args[2]
  2.0 1.0 %fusion.112 = (f32[216,256]{0,1:T(8,128)S(1)}, f32[216,256]{0,1:T(8,128)S(1)}) fusion(f32[216,256]{0,1:T(8,128)S(1)} %copy.5), kind=kLoop, calls=%fused_computation.210 | loop fusion | bytes 663552 | tf_op jit(solution)/shard_map/cos | solution.py:56
  3.0 1.6 %gather_fusion.4 = f32[512,216]{1,0:T(8,128)S(1)} fusion(f32[216,256]{0,1:T(8,128)S(1)} %get-tuple-element.16, s32[1024]{0:T(1024)S(1)} %pad_clamp_fusion), kind=kCustom, calls=%fused_computation.4.clone | custom fusion | bytes 886784 | tf_op jit(solution)/shard_map/jit(_take)/gather | solution.py:18
  4.8 1.6 %gather_fusion.5 = f32[512,216]{1,0:T(8,128)S(1)} fusion(f32[216,256]{0,1:T(8,128)S(1)} %get-tuple-element.17, s32[1024]{0:T(1024)S(1)} %pad_clamp_fusion), kind=kCustom, calls=%fused_computation.5.clone | custom fusion | bytes 886784 | tf_op jit(solution)/shard_map/jit(_take)/gather | solution.py:19
  6.6 0.8 %copy-done.11 = bf16[2,216,512]{2,1,0:T(8,128)(2,1)S(1)} copy-done((bf16[2,216,512]{2,1,0:T(8,128)(2,1)S(1)}, bf16[2,216,512]{2,1,0:T(8,128)(2,1)}, u32[]{:S(2)}) %copy-start.11) | copy-done | bytes 442392
  7.6 0.7 %fusion.66 = bf16[2,216,256]{2,1,0:T(8,128)(2,1)} fusion(s32[]{:T(128)S(6)} %select_n.70, bf16[1,216,512]{2,1,0:T(8,128)(2,1)S(1)} %get-tuple-element.15, bf16[1,216,512]{2,1,0:T(8,128)(2,1)S(1)} %get-tuple-element.14), kind=kLoop, calls=%fused_computation.135 | loop fusion | flops 442368 | bytes 663556 | tf_op jit(solution)/shard_map/stack | solution.py:22
  8.3 3.0 %collective-permute-start = (bf16[2,216,256]{2,1,0:T(8,128)(2,1)}, bf16[2,216,256]{2,1,0:T(8,128)(2,1)}, u32[]{:S(2)}, u32[]{:S(2)}) collective-permute-start(bf16[2,216,256]{2,1,0:T(8,128)(2,1)} %fusion.66), channel_id=1, source_target_pairs={{0,16},{16,0},{1,17},{17,1},{2,18},{18,2},{3,19},{19,3},{4,20},{20... | collective-permute-start | bytes 663560 | tf_op jit(solution)/shard_map/ppermute | solution.py:14
  11.3 1.6 %gather_fusion.6 = f32[512,216]{1,0:T(8,128)S(1)} fusion(f32[216,256]{0,1:T(8,128)S(1)} %get-tuple-element.17, s32[1024]{0:T(1024)S(1)} %pad_clamp_fusion.1), kind=kCustom, calls=%fused_computation.6.clone | custom fusion | bytes 886784 | tf_op jit(solution)/shard_map/jit(_take)/gather | solution.py:19
  12.9 1.6 %gather_fusion.3 = f32[512,216]{1,0:T(8,128)S(1)} fusion(f32[216,256]{0,1:T(8,128)S(1)} %get-tuple-element.16, s32[1024]{0:T(1024)S(1)} %pad_clamp_fusion.1), kind=kCustom, calls=%fused_computation.3.clone | custom fusion | bytes 886784 | tf_op jit(solution)/shard_map/jit(_take)/gather | solution.py:18
  14.5 1.6 %gather_fusion.7 = f32[512,216]{1,0:T(8,128)S(1)} fusion(f32[216,256]{0,1:T(8,128)S(1)} %get-tuple-element.17, s32[1024]{0:T(1024)S(1)} %pad_clamp_fusion.2), kind=kCustom, calls=%fused_computation.7.clone | custom fusion | bytes 886784 | tf_op jit(solution)/shard_map/jit(_take)/gather | solution.py:19
  16.1 1.6 %gather_fusion.2 = f32[512,216]{1,0:T(8,128)S(1)} fusion(f32[216,256]{0,1:T(8,128)S(1)} %get-tuple-element.16, s32[1024]{0:T(1024)S(1)} %pad_clamp_fusion.2), kind=kCustom, calls=%fused_computation.2.clone | custom fusion | bytes 886784 | tf_op jit(solution)/shard_map/jit(_take)/gather | solution.py:18
  17.7 2.2 %gather_fusion.8 = f32[512,216]{1,0:T(8,128)} fusion(f32[216,256]{0,1:T(8,128)S(1)} %get-tuple-element.17, s32[1024]{0:T(1024)S(1)} %pad_clamp_fusion.3), kind=kCustom, calls=%fused_computation.8.clone | custom fusion | bytes 886784 | tf_op jit(solution)/shard_map/jit(_take)/gather | solution.py:19
  19.9 2.2 %gather_fusion.1 = f32[512,216]{1,0:T(8,128)} fusion(f32[216,256]{0,1:T(8,128)S(1)} %get-tuple-element.16, s32[1024]{0:T(1024)S(1)} %pad_clamp_fusion.3), kind=kCustom, calls=%fused_computation.1.clone | custom fusion | bytes 886784 | tf_op jit(solution)/shard_map/jit(_take)/gather | solution.py:18
  22.2 2.2 %gather_fusion.9 = f32[512,216]{1,0:T(8,128)} fusion(f32[216,256]{0,1:T(8,128)S(1)} %get-tuple-element.17, s32[1024]{0:T(1024)S(1)} %pad_clamp_fusion.4), kind=kCustom, calls=%fused_computation.9.clone | custom fusion | bytes 886784 | tf_op jit(solution)/shard_map/jit(_take)/gather | solution.py:19
  24.4 2.2 %gather_fusion = f32[512,216]{1,0:T(8,128)} fusion(f32[216,256]{0,1:T(8,128)S(1)} %get-tuple-element.16, s32[1024]{0:T(1024)S(1)} %pad_clamp_fusion.4), kind=kCustom, calls=%fused_computation.clone | custom fusion | bytes 886784 | tf_op jit(solution)/shard_map/jit(_take)/gather | solution.py:18
  26.6 1.0 %fusion.81 = f32[2,256,216]{1,2,0:T(8,128)} fusion(bf16[2,2,216,216]{3,2,1,0:T(8,128)(2,1)S(1)} %copy-done, s32[]{:T(128)S(6)} %select_n.69, s32[]{:T(128)S(6)} %select_n.68, bf16[1,216,512]{2,1,0:T(8,128)(2,1)S(1)} %get-tuple-element.15, bf16[1,216,512]{2,1,0:T(8,128)(2,1)S(1)} %get-tuple-element.14), kind=kOutput, calls=%fused_computation.174 | convolution fusion | flops 48218112 | bytes 995336 | tf_op jit(solution)/shard_map/jk,rkh->rjh/dot_general | solution.py:32
  27.6 1.0 %fusion.80 = f32[2,256,216]{1,2,0:T(8,128)} fusion(bf16[2,2,216,216]{3,2,1,0:T(8,128)(2,1)S(1)} %copy-done, s32[]{:T(128)S(6)} %add.230, s32[]{:T(128)S(6)} %select_n.69, s32[]{:T(128)S(6)} %select_n.68, bf16[1,216,512]{2,1,0:T(8,128)(2,1)S(1)} %get-tuple-element.15, bf16[1,216,512]{2,1,0:T(8,128)(2,1)S(1)} %get-tuple-element.14), kind=kOutput, calls=%fused_computation.171 | convolution fusion | flops 48218112 | bytes 995340 | tf_op jit(solution)/shard_map/jk,rkh->rjh/dot_general | solution.py:32
  28.6 1.0 %copy.13 = f32[512,216]{0,1:T(8,128)} copy(f32[512,216]{1,0:T(8,128)S(1)} %gather_fusion.6) | data formatting | bytes 884736 | tf_op jit(solution)/shard_map/jit(_take)/gather | solution.py:19
  29.6 1.0 %copy.9 = f32[512,216]{0,1:T(8,128)} copy(f32[512,216]{1,0:T(8,128)S(1)} %gather_fusion.3) | data formatting | bytes 884736 | tf_op jit(solution)/shard_map/jit(_take)/gather | solution.py:18
  30.6 0.9 %copy.14 = f32[512,216]{0,1:T(8,128)} copy(f32[512,216]{1,0:T(8,128)S(1)} %gather_fusion.7) | data formatting | bytes 884736 | tf_op jit(solution)/shard_map/jit(_take)/gather | solution.py:19
  31.5 1.0 %copy.8 = f32[512,216]{0,1:T(8,128)} copy(f32[512,216]{1,0:T(8,128)S(1)} %gather_fusion.2) | data formatting | bytes 884736 | tf_op jit(solution)/shard_map/jit(_take)/gather | solution.py:18
  32.7 0.8 %copy-done.1 = f32[512,216]{1,0:T(8,128)S(1)} copy-done((f32[512,216]{1,0:T(8,128)S(1)}, f32[512,216]{1,0:T(8,128)}, u32[]{:S(2)}) %copy-start.1) | copy-done | bytes 442392
  33.8 0.8 %copy-done.3 = f32[512,216]{1,0:T(8,128)S(1)} copy-done((f32[512,216]{1,0:T(8,128)S(1)}, f32[512,216]{1,0:T(8,128)}, u32[]{:S(2)}) %copy-start.3) | copy-done | bytes 442392
  34.8 0.8 %copy-done.4 = f32[512,216]{1,0:T(8,128)S(1)} copy-done((f32[512,216]{1,0:T(8,128)S(1)}, f32[512,216]{1,0:T(8,128)}, u32[]{:S(2)}) %copy-start.4) | copy-done | bytes 442392
  35.9 0.8 %copy-done.5 = f32[2,256,216]{1,2,0:T(8,128)S(1)} copy-done((f32[2,256,216]{1,2,0:T(8,128)S(1)}, f32[2,256,216]{1,2,0:T(8,128)}, u32[]{:S(2)}) %copy-start.5) | copy-done | bytes 442392
  36.7 1.1 %fusion.19 = bf16[2,216,256]{2,1,0:T(8,128)(2,1)S(1)} fusion(f32[2,256,216]{1,2,0:T(8,128)S(1)} %copy-done.5, bf16[2,216,256]{2,1,0:T(8,128)(2,1)} %collective-permute-done, bf16[2,2,216,216]{3,2,1,0:T(8,128)(2,1)S(1)} %copy-done, s32[]{:T(128)S(6)} %select_n.71), kind=kOutput, calls=%fused_computation.39 | convolution fusion | flops 47996928 | bytes 995332 | tf_op jit(solution)/shard_map/jk,rkh->rjh/dot_general | solution.py:35
  37.9 1.2 %fusion.18 = bf16[2,216,256]{2,1,0:T(8,128)(2,1)S(1)} fusion(f32[2,256,216]{1,2,0:T(8,128)S(1)} %copy-done.6, bf16[2,216,256]{2,1,0:T(8,128)(2,1)} %collective-permute-done, bf16[2,2,216,216]{3,2,1,0:T(8,128)(2,1)S(1)} %copy-done, s32[]{:T(128)S(6)} %add.230, s32[]{:T(128)S(6)} %select_n.71), kind=kOutput, calls=%fused_computation.38 | convolution fusion | flops 47996928 | bytes 995336 | tf_op jit(solution)/shard_map/jk,rkh->rjh/dot_general | solution.py:35
  39.4 0.2 fusion.79
  39.7 0.2 fusion.78
  39.9 1.0 %collective-permute-done.1 = bf16[2,216,256]{2,1,0:T(8,128)(2,1)S(1)} collective-permute-done((bf16[2,216,256]{2,1,0:T(8,128)(2,1)S(1)}, bf16[2,216,256]{2,1,0:T(8,128)(2,1)S(1)}, u32[]{:S(2)}, u32[]{:S(2)}) %collective-permute-start.1) | collective-permute-done | bytes 221216 | tf_op jit(solution)/shard_map/ppermute | solution.py:14
  40.9 0.2 fusion.17
  41.1 0.2 fusion.16
  41.4 0.8 %copy-done.7 = f32[512,216]{0,1:T(8,128)S(1)} copy-done((f32[512,216]{0,1:T(8,128)S(1)}, f32[512,216]{0,1:T(8,128)}, u32[]{:S(2)}) %copy-start.7) | copy-done | bytes 442392
  42.5 1.6 %collective-permute-start.2 = (bf16[2,216,256]{2,1,0:T(8,128)(2,1)S(1)}, bf16[2,216,256]{2,1,0:T(8,128)(2,1)S(1)}, u32[]{:S(2)}, u32[]{:S(2)}) collective-permute-start(bf16[2,216,256]{2,1,0:T(8,128)(2,1)S(1)} %fusion.62), channel_id=1, source_target_pairs={{0,8},{8,0},{4,12},{12,4},{1,9},{9,1},{5,13},{13,5},{2,10},{10,2},... | collective-permute-start | bytes 663560 | tf_op jit(solution)/shard_map/ppermute | solution.py:14
  44.3 0.2 fusion.76
  44.5 5.5 %collective-permute-done.2 = bf16[2,216,256]{2,1,0:T(8,128)(2,1)S(1)} collective-permute-done((bf16[2,216,256]{2,1,0:T(8,128)(2,1)S(1)}, bf16[2,216,256]{2,1,0:T(8,128)(2,1)S(1)}, u32[]{:S(2)}, u32[]{:S(2)}) %collective-permute-start.2) | collective-permute-done | bytes 221216 | tf_op jit(solution)/shard_map/ppermute | solution.py:14
  50.0 0.2 fusion.15
  50.2 0.2 fusion.14
  50.7 1.6 %collective-permute-start.3 = (bf16[2,216,256]{2,1,0:T(8,128)(2,1)S(1)}, bf16[2,216,256]{2,1,0:T(8,128)(2,1)S(1)}, u32[]{:S(2)}, u32[]{:S(2)}) collective-permute-start(bf16[2,216,256]{2,1,0:T(8,128)(2,1)S(1)} %fusion.60), channel_id=1, source_target_pairs={{0,1},{1,0},{2,3},{3,2},{4,5},{5,4},{6,7},{7,6},{8,9},{9,8},{10,11... | collective-permute-start | bytes 663560 | tf_op jit(solution)/shard_map/ppermute | solution.py:14
  52.5 0.2 fusion.74
  52.8 4.6 %collective-permute-done.3 = bf16[2,216,256]{2,1,0:T(8,128)(2,1)S(1)} collective-permute-done((bf16[2,216,256]{2,1,0:T(8,128)(2,1)S(1)}, bf16[2,216,256]{2,1,0:T(8,128)(2,1)S(1)}, u32[]{:S(2)}, u32[]{:S(2)}) %collective-permute-start.3) | collective-permute-done | bytes 221216 | tf_op jit(solution)/shard_map/ppermute | solution.py:14
  57.6 0.2 fusion.12
  58.0 2.7 %collective-permute-start.4 = (bf16[2,216,256]{2,1,0:T(8,128)(2,1)S(1)}, bf16[2,216,256]{2,1,0:T(8,128)(2,1)S(1)}, u32[]{:S(2)}, u32[]{:S(2)}) collective-permute-start(bf16[2,216,256]{2,1,0:T(8,128)(2,1)S(1)} %fusion.58), channel_id=1, source_target_pairs={{0,2},{2,0},{1,3},{3,1},{4,6},{6,4},{5,7},{7,5},{8,10},{10,8},{9,1... | collective-permute-start | bytes 663560 | tf_op jit(solution)/shard_map/ppermute | solution.py:14
  60.9 0.2 fusion.72
  61.1 8.4 %collective-permute-done.4 = bf16[2,216,256]{2,1,0:T(8,128)(2,1)S(1)} collective-permute-done((bf16[2,216,256]{2,1,0:T(8,128)(2,1)S(1)}, bf16[2,216,256]{2,1,0:T(8,128)(2,1)S(1)}, u32[]{:S(2)}, u32[]{:S(2)}) %collective-permute-start.4) | collective-permute-done | bytes 221216 | tf_op jit(solution)/shard_map/ppermute | solution.py:14
  69.7 0.2 fusion.10
  69.9 0.8 %pad_maximum_fusion = bf16[2,216,512]{2,1,0:T(8,128)(2,1)} fusion(bf16[2,216,256]{2,1,0:T(8,128)(2,1)S(1)} %fusion.10, bf16[2,216,256]{2,1,0:T(8,128)(2,1)S(1)} %fusion.11), kind=kLoop, calls=%fused_computation.108 | loop fusion | flops 884736 | bytes 884736 | tf_op jit(solution)/shard_map/concatenate | solution.py:39
  (53 shorter events, 3.6 us)
Async XLA Ops:
  0.0 26.6 %copy-start = (bf16[2,2,216,216]{3,2,1,0:T(8,128)(2,1)S(1)}, bf16[2,2,216,216]{3,2,1,0:T(8,128)(2,1)}, u32[]{:S(2)}) copy-start(bf16[2,2,216,216]{3,2,1,0:T(8,128)(2,1)} %param.7) | copy-start | bytes 1119748
  6.4 1.0 %copy-start.11 = (bf16[2,216,512]{2,1,0:T(8,128)(2,1)S(1)}, bf16[2,216,512]{2,1,0:T(8,128)(2,1)}, u32[]{:S(2)}) copy-start(bf16[2,216,512]{2,1,0:T(8,128)(2,1)} %param.6) | copy-start | bytes 1327108
  8.3 27.6 %collective-permute-start = (bf16[2,216,256]{2,1,0:T(8,128)(2,1)}, bf16[2,216,256]{2,1,0:T(8,128)(2,1)}, u32[]{:S(2)}, u32[]{:S(2)}) collective-permute-start(bf16[2,216,256]{2,1,0:T(8,128)(2,1)} %fusion.66), channel_id=1, source_target_pairs={{0,16},{16,0},{1,17},{17,1},{2,18},{18,2},{3,19},{19,3},{4,20},{20... | collective-permute-start | bytes 663560 | tf_op jit(solution)/shard_map/ppermute | solution.py:14
  31.5 1.0 %copy-start.2 = (f32[512,216]{1,0:T(8,128)S(1)}, f32[512,216]{1,0:T(8,128)}, u32[]{:S(2)}) copy-start(f32[512,216]{1,0:T(8,128)} %gather_fusion.8) | copy-start | bytes 1327108
  32.5 1.0 %copy-start.1 = (f32[512,216]{1,0:T(8,128)S(1)}, f32[512,216]{1,0:T(8,128)}, u32[]{:S(2)}) copy-start(f32[512,216]{1,0:T(8,128)} %gather_fusion.1) | copy-start | bytes 1327108
  33.6 1.0 %copy-start.3 = (f32[512,216]{1,0:T(8,128)S(1)}, f32[512,216]{1,0:T(8,128)}, u32[]{:S(2)}) copy-start(f32[512,216]{1,0:T(8,128)} %gather_fusion.9) | copy-start | bytes 1327108
  34.6 1.0 %copy-start.4 = (f32[512,216]{1,0:T(8,128)S(1)}, f32[512,216]{1,0:T(8,128)}, u32[]{:S(2)}) copy-start(f32[512,216]{1,0:T(8,128)} %gather_fusion) | copy-start | bytes 1327108
  35.7 1.0 %copy-start.5 = (f32[2,256,216]{1,2,0:T(8,128)S(1)}, f32[2,256,216]{1,2,0:T(8,128)}, u32[]{:S(2)}) copy-start(f32[2,256,216]{1,2,0:T(8,128)} %fusion.81) | copy-start | bytes 1327108
  35.9 2.0 %copy-start.6 = (f32[2,256,216]{1,2,0:T(8,128)S(1)}, f32[2,256,216]{1,2,0:T(8,128)}, u32[]{:S(2)}) copy-start(f32[2,256,216]{1,2,0:T(8,128)} %fusion.80) | copy-start | bytes 1327108
  37.8 1.3 %copy-start.9 = (f32[512,216]{0,1:T(8,128)S(1)}, f32[512,216]{0,1:T(8,128)}, u32[]{:S(2)}) copy-start(f32[512,216]{0,1:T(8,128)} %copy.13) | copy-start | bytes 1327108
  37.9 1.3 %copy-start.10 = (f32[512,216]{0,1:T(8,128)S(1)}, f32[512,216]{0,1:T(8,128)}, u32[]{:S(2)}) copy-start(f32[512,216]{0,1:T(8,128)} %copy.9) | copy-start | bytes 1327108
  39.4 1.5 %collective-permute-start.1 = (bf16[2,216,256]{2,1,0:T(8,128)(2,1)S(1)}, bf16[2,216,256]{2,1,0:T(8,128)(2,1)S(1)}, u32[]{:S(2)}, u32[]{:S(2)}) collective-permute-start(bf16[2,216,256]{2,1,0:T(8,128)(2,1)S(1)} %fusion.64), channel_id=1, source_target_pairs={{0,4},{4,0},{8,12},{12,8},{1,5},{5,1},{9,13},{13,9},{2,6},{6,2},{1... | collective-permute-start | bytes 663560 | tf_op jit(solution)/shard_map/ppermute | solution.py:14
  41.1 1.0 %copy-start.7 = (f32[512,216]{0,1:T(8,128)S(1)}, f32[512,216]{0,1:T(8,128)}, u32[]{:S(2)}) copy-start(f32[512,216]{0,1:T(8,128)} %copy.14) | copy-start | bytes 1327108
  41.1 1.1 %copy-start.8 = (f32[512,216]{0,1:T(8,128)S(1)}, f32[512,216]{0,1:T(8,128)}, u32[]{:S(2)}) copy-start(f32[512,216]{0,1:T(8,128)} %copy.8) | copy-start | bytes 1327108
  42.5 7.5 %collective-permute-start.2 = (bf16[2,216,256]{2,1,0:T(8,128)(2,1)S(1)}, bf16[2,216,256]{2,1,0:T(8,128)(2,1)S(1)}, u32[]{:S(2)}, u32[]{:S(2)}) collective-permute-start(bf16[2,216,256]{2,1,0:T(8,128)(2,1)S(1)} %fusion.62), channel_id=1, source_target_pairs={{0,8},{8,0},{4,12},{12,4},{1,9},{9,1},{5,13},{13,5},{2,10},{10,2},... | collective-permute-start | bytes 663560 | tf_op jit(solution)/shard_map/ppermute | solution.py:14
  50.7 6.7 %collective-permute-start.3 = (bf16[2,216,256]{2,1,0:T(8,128)(2,1)S(1)}, bf16[2,216,256]{2,1,0:T(8,128)(2,1)S(1)}, u32[]{:S(2)}, u32[]{:S(2)}) collective-permute-start(bf16[2,216,256]{2,1,0:T(8,128)(2,1)S(1)} %fusion.60), channel_id=1, source_target_pairs={{0,1},{1,0},{2,3},{3,2},{4,5},{5,4},{6,7},{7,6},{8,9},{9,8},{10,11... | collective-permute-start | bytes 663560 | tf_op jit(solution)/shard_map/ppermute | solution.py:14
  58.0 11.5 %collective-permute-start.4 = (bf16[2,216,256]{2,1,0:T(8,128)(2,1)S(1)}, bf16[2,216,256]{2,1,0:T(8,128)(2,1)S(1)}, u32[]{:S(2)}, u32[]{:S(2)}) collective-permute-start(bf16[2,216,256]{2,1,0:T(8,128)(2,1)S(1)} %fusion.58), channel_id=1, source_target_pairs={{0,2},{2,0},{1,3},{3,1},{4,6},{6,4},{5,7},{7,5},{8,10},{10,8},{9,1... | collective-permute-start | bytes 663560 | tf_op jit(solution)/shard_map/ppermute | solution.py:14
where the time goes:
time: 71.2 us; the launch traced here: 70.7 us
  local copies, waits for them, and re-layouts  31.4 us (44%)
  waiting for transfers between devices  19.5 us (27%)
  starting transfers between devices  8.91 us (13%)
  matrix products  7.78 us (11%)
  other arithmetic  2.62 us (4%)
    ppermute x5, waiting for transfers between devices, swapped(): return lax.ppermute(block, axis, route)  19.5 us
    gather x10, local copies, waits for them, and re-layouts, rotate(): sines = jnp.take(sin_tab, labels, axis=1)  11.7 us
    gather x10, local copies, waits for them, and re-layouts, rotate(): cosines = jnp.take(cos_tab, labels, axis=1)  11.6 us
    ppermute x5, starting transfers between devices, swapped(): return lax.ppermute(block, axis, route)  8.91 us
    unnamed x25, local copies, waits for them, and re-layouts  6.23 us
    dot_general x10, matrix products, combine(): jnp.einsum('jk,rkh->rjh', far_mats[target], received, preferred_element_t...  4.09 us
    dot_general x10, matrix products, combine(): jnp.einsum('jk,rkh->rjh', own_mats[target], kept_half, preferred_element_...  3.69 us
    another operation x10, other arithmetic, rotate(): jnp.stack([cosines * real_part - sines * imag_part, sines * real_part + c...  1.75 us
  transfers between devices with their start and end apart: 5, of which 4 were waited for; matrix products, arithmetic and copies ran while one was open for 33% of the time, Pallas kernels for 0%

commit v1 on v0

v1 whole, which is shorter than its diff:
```python
import functools

import jax
import jax.numpy as jnp
from jax import lax
from jax.experimental import pallas as pl
from jax.experimental.pallas import tpu as pltpu
from jax.sharding import PartitionSpec as P

AXES = ("gx", "gy", "gz")
MESH = pl.DeviceIdType.MESH
LANES = 128


def sin_cos(x):
    turn = jnp.floor(x * 0.6366197723675814 + 0.5)
    r = (x - turn * 1.5703125) - turn * 4.838267948966e-4
    z = r * r
    s = r + r * z * (-1.6666654611e-1 + z * (8.3321608736e-3 - z * 1.9515295891e-4))
    c = 1.0 - 0.5 * z + z * z * (4.166664568298827e-2 + z * (-1.388731625493765e-3 + z * 2.443315711809948e-5))
    far = jnp.abs(turn)
    odd = far == 1.0
    sign = jnp.where(far == 2.0, -1.0, 1.0)
    return jnp.where(odd, turn * c, sign * s), jnp.where(odd, -turn * s, sign * c)


def kernel(stages, w_hbm, t_hbm, a_hbm, id_hbm, out, w, mats, ang, ids, cos_tab, sin_tab, cosg, sing,
           send, recv, kept, part, load_sem, send_sem, recv_sem):
    levels = len(stages)
    half = w.shape[2] // 2
    chunks = half // LANES
    boxes = ang.shape[1]

    loads = [pltpu.make_async_copy(src, dst, load_sem.at[n])
             for n, (src, dst) in enumerate(((a_hbm, ang), (id_hbm, ids), (w_hbm, w), (t_hbm, mats)))]
    for load in loads:
        load.start()

    parity, partner = [], []
    for axis, span in stages:
        me = lax.axis_index(axis)
        bit = (me // span) % 2
        parity.append(bit)
        partner.append({axis: me + (1 - 2 * bit) * span})

    barrier = pltpu.get_barrier_semaphore()
    for peer in partner:
        pl.semaphore_signal(barrier, inc=1, device_id=peer, device_id_type=MESH)

    def exchange(level, c):
        return pltpu.make_async_remote_copy(
            src_ref=send.at[level, c], dst_ref=recv.at[level, c],
            send_sem=send_sem.at[level, c], recv_sem=recv_sem.at[level, c],
            device_id=partner[level], device_id_type=MESH)

    def gather(level, h):
        row = ids[level:level + 1, pl.ds(pl.multiple_of(h * half, LANES), half)]
        hot = jnp.where(lax.broadcasted_iota(jnp.int32, (boxes, half), 0) == row, 1.0, 0.0).astype(jnp.bfloat16)
        c_all = jnp.dot(cos_tab[...], hot, preferred_element_type=jnp.float32).astype(jnp.bfloat16)
        s_all = jnp.dot(sin_tab[...], hot, preferred_element_type=jnp.float32).astype(jnp.bfloat16)
        for c in range(chunks):
            cosg[level, h, c] = c_all[:, c * LANES:(c + 1) * LANES]
            sing[level, h, c] = s_all[:, c * LANES:(c + 1) * LANES]

    def rotate(level, h, c, re, im):
        co = cosg[level, h, c].astype(jnp.float32)
        si = sing[level, h, c].astype(jnp.float32)
        return (co * re - si * im).astype(jnp.bfloat16), (si * re + co * im).astype(jnp.bfloat16)

    def put(ref, pair):
        ref[:, :LANES] = pair[0]
        ref[:, LANES:] = pair[1]

    def near(level, c):
        for t in range(2):
            part[c, t] = jnp.dot(mats[t, parity[level]], kept[c], preferred_element_type=jnp.float32)

    def first(h, c):
        cols = pl.ds(pl.multiple_of(h * half + c * LANES, LANES), LANES)
        return rotate(0, h, c, w[0, :, cols].astype(jnp.float32), w[1, :, cols].astype(jnp.float32))

    loads[0].wait()
    sin_v, cos_v = sin_cos(ang[...])
    sin_tab[...] = sin_v.astype(jnp.bfloat16)
    cos_tab[...] = cos_v.astype(jnp.bfloat16)
    loads[1].wait()
    gather(0, 1 - parity[0])
    loads[2].wait()
    for c in range(chunks):
        put(send.at[0, c], first(1 - parity[0], c))
        if c == 0:
            pl.semaphore_wait(barrier, levels)
        exchange(0, c).start()
    gather(0, parity[0])
    loads[3].wait()
    for c in range(chunks):
        put(kept.at[c], first(parity[0], c))
        near(0, c)
    for level in range(1, levels):
        for h in range(2):
            gather(level, h)

    for level in range(levels):
        for c in range(chunks):
            exchange(level, c).wait_recv()
            far = 1 - parity[level]

            def mixed(t):
                y = part[c, t] + jnp.dot(mats[t, far], recv[level, c], preferred_element_type=jnp.float32)
                return y[:, :LANES], y[:, LANES:]

            if level + 1 < levels:
                keep = parity[level + 1]
                put(send.at[level + 1, c], rotate(level + 1, 1 - keep, c, *mixed(1 - keep)))
                exchange(level + 1, c).start()
                put(kept.at[c], rotate(level + 1, keep, c, *mixed(keep)))
                near(level + 1, c)
            else:
                for t in range(2):
                    re, im = mixed(t)
                    cols = slice(t * half + c * LANES, t * half + (c + 1) * LANES)
                    out[0, :, cols] = re.astype(out.dtype)
                    out[1, :, cols] = im.astype(out.dtype)
    for level in range(levels):
        for c in range(chunks):
            exchange(level, c).wait_send()


def shards(stages, weights, translate, angles, box_ids):
    points, cols = weights.shape[1:]
    levels, chunks = len(stages), cols // 2 // LANES
    bf16 = jnp.bfloat16
    return pl.pallas_call(
        functools.partial(kernel, stages),
        out_shape=jax.ShapeDtypeStruct(weights.shape, weights.dtype),
        in_specs=[pl.BlockSpec(memory_space=pl.ANY)] * 4,
        out_specs=pl.BlockSpec(memory_space=pltpu.VMEM),
        scratch_shapes=[
            pltpu.VMEM(weights.shape, bf16),
            pltpu.VMEM(translate.shape, bf16),
            pltpu.VMEM(angles.shape, jnp.float32),
            pltpu.VMEM(box_ids.shape, jnp.int32),
            pltpu.VMEM(angles.shape, bf16),
            pltpu.VMEM(angles.shape, bf16),
            pltpu.VMEM((levels, 2, chunks, points, LANES), bf16),
            pltpu.VMEM((levels, 2, chunks, points, LANES), bf16),
            pltpu.VMEM((levels, chunks, points, 2 * LANES), bf16),
            pltpu.VMEM((levels, chunks, points, 2 * LANES), bf16),
            pltpu.VMEM((chunks, points, 2 * LANES), bf16),
            pltpu.VMEM((chunks, 2, points, 2 * LANES), jnp.float32),
            pltpu.SemaphoreType.DMA((4,)),
            pltpu.SemaphoreType.DMA((levels, chunks)),
            pltpu.SemaphoreType.DMA((levels, chunks)),
        ],
        compiler_params=pltpu.CompilerParams(collective_id=0, has_side_effects=True),
    )(weights, translate, angles, box_ids)


def solution(mesh):
    stages = [(axis, 1 << b) for axis in AXES for b in range(mesh.shape[axis].bit_length() - 1)]
    in_specs = (P(None, None, AXES), P(), P(), P(None, AXES))
    return jax.shard_map(functools.partial(shards, stages), mesh=mesh, in_specs=in_specs,
                         out_specs=P(None, None, AXES), check_vma=False)
```

time: 71.2 us -> 35.8 us (0.50)
  Pallas kernels: 0 us -> 33.8 us
  local copies, waits for them, and re-layouts: 31.4 us -> 1.8 us
  waiting for transfers between devices: 19.5 us -> 0 us
  starting transfers between devices: 8.91 us -> 0 us
  matrix products: 7.78 us -> 0 us
  other arithmetic: 2.62 us -> 0 us
    pallas_call x0 -> x1, Pallas kernels: none -> 33.8 us  [shards(): pl.pallas_call(functools.partial(kernel, stages), out_shape=jax.ShapeDtyp...]
    gather x20 -> x0, local copies, waits for them, and re-layouts: 23.3 us -> none  [the longest x10 11.7 us: rotate(): sines = jnp.take(sin_tab, labels, axis=1)]
    ppermute x5 -> x0, waiting for transfers between devices: 19.5 us -> none  [swapped(): return lax.ppermute(block, axis, route)]
    ppermute x5 -> x0, starting transfers between devices: 8.91 us -> none  [swapped(): return lax.ppermute(block, axis, route)]
    dot_general x20 -> x0, matrix products: 7.78 us -> none  [the longest x10 4.09 us: combine(): jnp.einsum('jk,rkh->rjh', far_mats[target], received, preferred_element_t...]
    unnamed x25 -> x1, local copies, waits for them, and re-layouts: 6.23 us -> 1.8 us
    another operation x10 -> x0, other arithmetic: 1.75 us -> none  [rotate(): jnp.stack([cosines * real_part - sines * imag_part, sines * real_part + c...]
    cos x1 -> x0, local copies, waits for them, and re-layouts: 0.97 us -> none  [shards(): cos_tab = jnp.cos(angles)]
  transfers between devices with their start and end apart: 5 -> 0, of which waited for: 4 -> 0; matrix products, arithmetic and copies ran while one was open for 33% -> 0% of each run, Pallas kernels for 0% -> 0%
where the time goes in v1:
time: 35.8 us; the launch traced here: 35.6 us
  Pallas kernels  33.8 us (94%)
  local copies, waits for them, and re-layouts  1.8 us (5%)
    pallas_call x1, Pallas kernels, shards(): pl.pallas_call(functools.partial(kernel, stages), out_shape=jax.ShapeDtyp...  33.8 us
    unnamed x1, local copies, waits for them, and re-layouts  1.8 us

profile of v1, /device:TPU:0, one launch (start us, length us, event | category | flops | bytes accessed | tf_op | source)
XLA Modules:
  0.0 35.6 jit_solution(9540995302187450719)
XLA Ops:
  0.0 33.8 %shard_map.46 = bf16[2,216,512]{2,1,0:T(8,128)(2,1)} custom-call(bf16[2,216,512]{2,1,0:T(8,128)(2,1)} %w_hbm.1, bf16[2,2,216,216]{3,2,1,0:T(8,128)(2,1)} %t_hbm.1, f32[216,256]{1,0:T(8,128)} %a_hbm.1, s32[5,512]{1,0:T(8,128)} %id_hbm.1), custom_call_target="tpu_custom_call" | custom-call | tf_op jit(solution)/shard_map/pallas_call | solution.py:133
  33.8 1.8 %copy.6 = bf16[2,216,512]{2,1,0:T(8,128)(2,1)} copy(bf16[2,216,512]{2,1,0:T(8,128)(2,1)} %shard_map.46) | data formatting | bytes 884736

commit v2 on v1

--- a/solution.py
+++ b/solution.py
@@ -132,7 +132,7 @@
     bf16 = jnp.bfloat16
     return pl.pallas_call(
         functools.partial(kernel, stages),
-        out_shape=jax.ShapeDtypeStruct(weights.shape, weights.dtype),
+        out_shape=pltpu.VMEM(weights.shape, weights.dtype),
         in_specs=[pl.BlockSpec(memory_space=pl.ANY)] * 4,
         out_specs=pl.BlockSpec(memory_space=pltpu.VMEM),
         scratch_shapes=[

time: 35.8 us -> 34 us (0.950)
  local copies, waits for them, and re-layouts: 1.8 us -> 0.76 us
  Pallas kernels: 33.8 us -> 33.1 us
    unnamed x1, local copies, waits for them, and re-layouts: 1.8 us -> 0.76 us
    pallas_call x1, Pallas kernels: 33.8 us -> 33.1 us  [shards(): pl.pallas_call(functools.partial(kernel, stages), out_shape=pltpu.VMEM(we...]
where the time goes in v2:
time: 34 us; the launch traced here: 33.8 us
  Pallas kernels  33.1 us (97%)
  local copies, waits for them, and re-layouts  0.76 us (2%)
    pallas_call x1, Pallas kernels, shards(): pl.pallas_call(functools.partial(kernel, stages), out_shape=pltpu.VMEM(we...  33.1 us
    unnamed x1, local copies, waits for them, and re-layouts  0.76 us

profile of v2, /device:TPU:0, one launch (start us, length us, event | category | flops | bytes accessed | tf_op | source)
XLA Modules:
  0.0 33.8 jit_solution(10126671146605464870)
XLA Ops:
  0.0 33.1 %shard_map.46 = bf16[2,216,512]{2,1,0:T(8,128)(2,1)S(1)} custom-call(bf16[2,216,512]{2,1,0:T(8,128)(2,1)} %w_hbm.1, bf16[2,2,216,216]{3,2,1,0:T(8,128)(2,1)} %t_hbm.1, f32[216,256]{1,0:T(8,128)} %a_hbm.1, s32[5,512]{1,0:T(8,128)} %id_hbm.1), custom_call_target="tpu_custom_call" | custom-call | tf_op jit(solution)/shard_map/pallas_call | solution.py:133
  33.1 0.8 %copy.6 = bf16[2,216,512]{2,1,0:T(8,128)(2,1)} copy(bf16[2,216,512]{2,1,0:T(8,128)(2,1)S(1)} %shard_map.46) | data formatting | bytes 884736

commit v3 on v2

v3 whole, which is shorter than its diff:
```python
import functools

import jax
import jax.numpy as jnp
from jax import lax
from jax.experimental import pallas as pl
from jax.experimental.pallas import tpu as pltpu
from jax.sharding import PartitionSpec as P

AXES = ("gx", "gy", "gz")
MESH = pl.DeviceIdType.MESH
LANES = 128
WIDTH = LANES // 2


def sin_cos(x):
    turn = jnp.floor(x * 0.6366197723675814 + 0.5)
    r = (x - turn * 1.5703125) - turn * 4.838267948966e-4
    z = r * r
    s = r + r * z * (-1.6666654611e-1 + z * (8.3321608736e-3 - z * 1.9515295891e-4))
    c = 1.0 - 0.5 * z + z * z * (4.166664568298827e-2 + z * (-1.388731625493765e-3 + z * 2.443315711809948e-5))
    far = jnp.abs(turn)
    odd = far == 1.0
    sign = jnp.where(far == 2.0, -1.0, 1.0)
    return jnp.where(odd, turn * c, sign * s), jnp.where(odd, -turn * s, sign * c)


def kernel(stages, w_hbm, t_hbm, a_hbm, id_hbm, out, w, mats, ang, ids, cos_tab, sin_tab, cosg, sing,
           send, recv, kept, part, load_sem, send_sem, recv_sem):
    levels = len(stages)
    half = w.shape[2] // 2
    points, boxes = ang.shape
    chunks = half // WIDTH

    loads = [pltpu.make_async_copy(src, dst, load_sem.at[n])
             for n, (src, dst) in enumerate(((a_hbm, ang), (id_hbm, ids), (w_hbm, w), (t_hbm, mats)))]
    for load in loads:
        load.start()

    parity, partner = [], []
    for axis, span in stages:
        me = lax.axis_index(axis)
        bit = (me // span) % 2
        parity.append(bit)
        partner.append({axis: me + (1 - 2 * bit) * span})

    barrier = pltpu.get_barrier_semaphore()
    for peer in partner:
        pl.semaphore_signal(barrier, inc=1, device_id=peer, device_id_type=MESH)

    def low(rows):
        return lax.broadcasted_iota(jnp.int32, (rows, LANES), 1) < WIDTH

    def swap(x):
        return pltpu.roll(x, WIDTH, 1)

    def exchange(level, q):
        return pltpu.make_async_remote_copy(
            src_ref=send.at[level, q], dst_ref=recv.at[level, q],
            send_sem=send_sem.at[level, q], recv_sem=recv_sem.at[level, q],
            device_id=partner[level], device_id_type=MESH)

    def columns(h, g):
        return pl.ds(pl.multiple_of(h * half + g * LANES, LANES), LANES)

    def gather(level, h, groups):
        rows = []
        for g in groups:
            row = jnp.broadcast_to(ids[level:level + 1, columns(h, g)], (8, LANES))
            turned = swap(row)
            rows += [jnp.where(low(8), row, turned)[:1], jnp.where(low(8), turned, row)[:1]]
        row = jnp.concatenate(rows, axis=1)
        hot = jnp.where(lax.broadcasted_iota(jnp.int32, (boxes, row.shape[1]), 0) == row, 1.0, 0.0).astype(jnp.bfloat16)
        c_all = jnp.dot(cos_tab[...], hot, preferred_element_type=jnp.float32)
        s_all = jnp.dot(sin_tab[...], hot, preferred_element_type=jnp.float32)
        for n in range(len(rows)):
            q = 2 * groups[0] + n
            cols = slice(n * LANES, (n + 1) * LANES)
            cosg[level, h, q] = c_all[:, cols].astype(jnp.bfloat16)
            sing[level, h, q] = jnp.where(low(points), -s_all[:, cols], s_all[:, cols]).astype(jnp.bfloat16)

    def rotate(level, h, q, x):
        co = cosg[level, h, q].astype(jnp.float32)
        si = sing[level, h, q].astype(jnp.float32)
        return (co * x + si * swap(x)).astype(jnp.bfloat16)

    def near(level, q):
        for t in range(2):
            part[q, t] = jnp.dot(mats[t, parity[level]], kept[q], preferred_element_type=jnp.float32)

    def first(h, g):
        re = w[0, :, columns(h, g)].astype(jnp.float32)
        im = w[1, :, columns(h, g)].astype(jnp.float32)
        pair = jnp.where(low(points), re, swap(im)), jnp.where(low(points), swap(re), im)
        return [(2 * g + side, rotate(0, h, 2 * g + side, x)) for side, x in enumerate(pair)]

    groups = list(range(chunks // 2))
    loads[0].wait()
    sin_v, cos_v = sin_cos(ang[...])
    sin_tab[...] = sin_v.astype(jnp.bfloat16)
    cos_tab[...] = cos_v.astype(jnp.bfloat16)
    loads[1].wait()
    for g in groups:
        gather(0, 1 - parity[0], [g])
        if g == 0:
            loads[2].wait()
        for q, x in first(1 - parity[0], g):
            send[0, q] = x
        if g == 0:
            pl.semaphore_wait(barrier, levels)
        for side in range(2):
            exchange(0, 2 * g + side).start()
    gather(0, parity[0], groups)
    loads[3].wait()
    for g in groups:
        for q, x in first(parity[0], g):
            kept[q] = x
            near(0, q)
    for level in range(1, levels):
        for h in range(2):
            gather(level, h, groups)

    ready = set()
    for level, q in [(level, q) for level in range(levels) for q in range(chunks)]:
        far = 1 - parity[level]
        exchange(level, q).wait_recv()

        def mixed(t):
            return part[q, t] + jnp.dot(mats[t, far], recv[level, q], preferred_element_type=jnp.float32)

        if level + 1 < levels:
            keep = parity[level + 1]
            send[level + 1, q] = rotate(level + 1, 1 - keep, q, mixed(1 - keep))
            exchange(level + 1, q).start()
            kept[q] = rotate(level + 1, keep, q, mixed(keep))
            near(level + 1, q)
        else:
            for t in range(2):
                y = mixed(t)
                if q ^ 1 in ready:
                    other = part[q ^ 1, t]
                    a, b = (other, y) if q % 2 else (y, other)
                    cols = slice(t * half + q // 2 * LANES, t * half + (q // 2 + 1) * LANES)
                    out[0, :, cols] = jnp.where(low(points), a, swap(b)).astype(out.dtype)
                    out[1, :, cols] = jnp.where(low(points), swap(a), b).astype(out.dtype)
                else:
                    part[q, t] = y
            ready.add(q)
    for level in range(levels):
        for q in range(chunks):
            exchange(level, q).wait_send()


def shards(stages, weights, translate, angles, box_ids):
    points, cols = weights.shape[1:]
    levels, chunks = len(stages), cols // 2 // WIDTH
    bf16 = jnp.bfloat16
    return pl.pallas_call(
        functools.partial(kernel, stages),
        out_shape=pltpu.VMEM(weights.shape, weights.dtype),
        in_specs=[pl.BlockSpec(memory_space=pl.ANY)] * 4,
        out_specs=pl.BlockSpec(memory_space=pltpu.VMEM),
        scratch_shapes=[
            pltpu.VMEM(weights.shape, bf16),
            pltpu.VMEM(translate.shape, bf16),
            pltpu.VMEM(angles.shape, jnp.float32),
            pltpu.VMEM(box_ids.shape, jnp.int32),
            pltpu.VMEM(angles.shape, bf16),
            pltpu.VMEM(angles.shape, bf16),
            pltpu.VMEM((levels, 2, chunks, points, LANES), bf16),
            pltpu.VMEM((levels, 2, chunks, points, LANES), bf16),
            pltpu.VMEM((levels, chunks, points, LANES), bf16),
            pltpu.VMEM((levels, chunks, points, LANES), bf16),
            pltpu.VMEM((chunks, points, LANES), bf16),
            pltpu.VMEM((chunks, 2, points, LANES), jnp.float32),
            pltpu.SemaphoreType.DMA((4,)),
            pltpu.SemaphoreType.DMA((levels, chunks)),
            pltpu.SemaphoreType.DMA((levels, chunks)),
        ],
        compiler_params=pltpu.CompilerParams(collective_id=0, has_side_effects=True),
    )(weights, translate, angles, box_ids)


def solution(mesh):
    stages = [(axis, 1 << b) for axis in AXES for b in range(mesh.shape[axis].bit_length() - 1)]
    in_specs = (P(None, None, AXES), P(), P(), P(None, AXES))
    return jax.shard_map(functools.partial(shards, stages), mesh=mesh, in_specs=in_specs,
                         out_specs=P(None, None, AXES), check_vma=False)
```

time: 34 us -> 32.5 us (0.956)
  Pallas kernels: 33.1 us -> 31.6 us
    pallas_call x1, Pallas kernels: 33.1 us -> 31.6 us  [shards(): pl.pallas_call(functools.partial(kernel, stages), out_shape=pltpu.VMEM(we...]
where the time goes in v3:
time: 32.5 us; the launch traced here: 32.4 us
  Pallas kernels  31.6 us (97%)
  local copies, waits for them, and re-layouts  0.76 us (2%)
    pallas_call x1, Pallas kernels, shards(): pl.pallas_call(functools.partial(kernel, stages), out_shape=pltpu.VMEM(we...  31.6 us
    unnamed x1, local copies, waits for them, and re-layouts  0.76 us

profile of v3, /device:TPU:0, one launch (start us, length us, event | category | flops | bytes accessed | tf_op | source)
XLA Modules:
  0.0 32.4 jit_solution(1177456729844824941)
XLA Ops:
  0.0 31.6 %shard_map.46 = bf16[2,216,512]{2,1,0:T(8,128)(2,1)S(1)} custom-call(bf16[2,216,512]{2,1,0:T(8,128)(2,1)} %w_hbm.1, bf16[2,2,216,216]{3,2,1,0:T(8,128)(2,1)} %t_hbm.1, f32[216,256]{1,0:T(8,128)} %a_hbm.1, s32[5,512]{1,0:T(8,128)} %id_hbm.1), custom_call_target="tpu_custom_call" | custom-call | tf_op jit(solution)/shard_map/pallas_call | solution.py:158
  31.6 0.8 %copy.6 = bf16[2,216,512]{2,1,0:T(8,128)(2,1)} copy(bf16[2,216,512]{2,1,0:T(8,128)(2,1)S(1)} %shard_map.46) | data formatting | bytes 884736

commit v4 on v3

--- a/solution.py
+++ b/solution.py
@@ -121,7 +121,8 @@
             gather(level, h, groups)
 
     ready = set()
-    for level, q in [(level, q) for level in range(levels) for q in range(chunks)]:
+    steps = [(level, q) for level in range(levels) for q in range(chunks)]
+    for level, q in sorted(steps, key=lambda step: (2 * step[0] + step[1], -step[0])):
         far = 1 - parity[level]
         exchange(level, q).wait_recv()
 

time: 32.5 us -> 30.9 us (0.951)
  Pallas kernels: 31.6 us -> 30 us
    pallas_call x1, Pallas kernels: 31.6 us -> 30 us  [shards(): pl.pallas_call(functools.partial(kernel, stages), out_shape=pltpu.VMEM(we...]
where the time goes in v4:
time: 30.9 us; the launch traced here: 30.7 us
  Pallas kernels  30 us (97%)
  local copies, waits for them, and re-layouts  0.76 us (2%)
    pallas_call x1, Pallas kernels, shards(): pl.pallas_call(functools.partial(kernel, stages), out_shape=pltpu.VMEM(we...  30 us
    unnamed x1, local copies, waits for them, and re-layouts  0.76 us

profile of v4, /device:TPU:0, one launch (start us, length us, event | category | flops | bytes accessed | tf_op | source)
XLA Modules:
  0.0 30.7 jit_solution(8989642844423788139)
XLA Ops:
  0.0 30.0 %shard_map.46 = bf16[2,216,512]{2,1,0:T(8,128)(2,1)S(1)} custom-call(bf16[2,216,512]{2,1,0:T(8,128)(2,1)} %w_hbm.1, bf16[2,2,216,216]{3,2,1,0:T(8,128)(2,1)} %t_hbm.1, f32[216,256]{1,0:T(8,128)} %a_hbm.1, s32[5,512]{1,0:T(8,128)} %id_hbm.1), custom_call_target="tpu_custom_call" | custom-call | tf_op jit(solution)/shard_map/pallas_call | solution.py:159
  30.0 0.8 %copy.6 = bf16[2,216,512]{2,1,0:T(8,128)(2,1)} copy(bf16[2,216,512]{2,1,0:T(8,128)(2,1)S(1)} %shard_map.46) | data formatting | bytes 884736
